TPU v7x, 256 devices: a whole 4x4x8 slice. The times are simulated.
256 devices in a mesh: freq: 32 (over y_hi, z, core), tm: 4 (over x), grp: 2 (over y_lo).
Axes of the slice: x: 4, y: 4 (y_hi: 2, y_lo: 2; y = y_hi * 2 + y_lo), z: 8, core: 2. Of those that a mesh axis runs over, the one named last changes fastest.
Arguments:
- voltages: bfloat16 [32, 2, 1024, 4096], P(None, None, ('freq', 'grp'), 'tm'), may hold values from -6 to 6
- prior_gains: float32 [32, 2, 1024], P('freq'), may hold values from -4.2 to 4.2
- station_flags: int32 [512], replicated, may hold values 0 or 1
- ingest_map: int32 [512], replicated, may hold values from 0 to 511, each once
- station_coords: float32 [2, 512], replicated, may hold values from -40 to 40
- pointing: int32 [2, 256], replicated, may hold values from 0 to 63
- corr_channels: int32 [32], replicated, may hold values from 0 to 31, each once
- beam_channels: int32 [32], replicated, may hold values from 0 to 31, each once
Outputs:
- visibilities: float32 [32, 2, 1024, 1024], P('freq', None, 'grp', 'tm')
- solved_gains: float32 [32, 2, 1024], P('freq')
- tied_beams: bfloat16 [32, 2, 2, 256, 4096], P('freq', None, None, 'grp', 'tm')
Inputs may be any that keep to these rules, and one draw needn't show every extreme that they name: `ingest_map`: each station appears in exactly one ingest slot. `corr_channels`: each channel is handled by exactly one correlator slot. `beam_channels`: each channel is handled by exactly one beamformer slot.
All inputs are finite; a program needn't handle non-finite values.
Results may differ from a plain program's by a relative error of at most 0.0049.
Values may be sent and summed in bfloat16 or wider, within the bound.
No kernel may reach another device: no remote copies, remote signals or barrier semaphores. Data moves between devices by JAX's collectives and lax.ppermute only.
A program may use at most 64 MiB of HBM per device.

v0:
```python
import math
import jax
import jax.numpy as jnp
from jax import lax
from jax.sharding import PartitionSpec as P

S = 512
ITERS = 4
grid_cells = 64.0


def weights_for(gains_sel, ratio, pointing_part, slot_coords):
    east_dir = (pointing_part[0].astype(jnp.float32) + 0.5) / grid_cells - 0.5
    north_dir = (pointing_part[1].astype(jnp.float32) + 0.5) / grid_cells - 0.5
    phase = (
        2.0
        * math.pi
        * ratio
        * (
            east_dir[:, None] * slot_coords[0][None, :]
            + north_dir[:, None] * slot_coords[1][None, :]
        )
    )
    cosine = jnp.cos(phase)
    sine = jnp.sin(phase)
    gain_real = gains_sel[0].reshape(2, S)
    gain_imag = gains_sel[1].reshape(2, S)
    denom = jnp.maximum(gain_real * gain_real + gain_imag * gain_imag, 0.5)
    along_real = gain_real / denom
    along_imag = gain_imag / denom
    factor = 1.0 / math.sqrt(S)
    w_real = (cosine[None] * along_real[:, None, :] - sine[None] * along_imag[:, None, :]) * factor
    w_imag = -(cosine[None] * along_imag[:, None, :] + sine[None] * along_real[:, None, :]) * factor
    upper = jnp.stack([w_real, -w_imag], axis=2)
    lower = jnp.stack([w_imag, w_real], axis=2)
    return jnp.stack([upper, lower], axis=1).astype(jnp.bfloat16)


def body(
    voltages,
    prior_gains,
    station_flags,
    ingest_map,
    station_coords,
    pointing,
    corr_channels,
    beam_channels,
):
    highest = lax.Precision.HIGHEST
    n_freq = lax.axis_size("freq")
    n_time = lax.axis_size("tm")
    n_group = lax.axis_size("grp")
    freq_index = lax.axis_index("freq")
    time_index = lax.axis_index("tm")
    group_index = lax.axis_index("grp")
    channels_all = voltages.shape[0]
    per_device = channels_all // n_freq
    samples = voltages.shape[3]
    inputs_all = 2 * S
    paired = lax.all_gather(voltages, "grp", axis=2, tiled=True)
    corr_source = jnp.take(paired, corr_channels, axis=0)
    beam_source = jnp.take(paired, beam_channels, axis=0)
    corr_volts, beam_volts = (
        lax.all_to_all(corr_source, "freq", split_axis=0, concat_axis=2, tiled=True),
        lax.all_to_all(beam_source, "freq", split_axis=0, concat_axis=2, tiled=True),
    )
    slot_keep = 1 - jnp.take(station_flags, ingest_map)
    keep = jnp.concatenate([slot_keep, slot_keep]).astype(jnp.bfloat16)
    corr_volts = corr_volts * keep[None, None, :, None]
    beam_volts = beam_volts * keep[None, None, :, None]
    rows = inputs_all // n_group
    row_start = group_index * rows
    mine = lax.dynamic_slice_in_dim(corr_volts, row_start, rows, 2)
    left = jnp.stack([mine, jnp.stack([mine[:, 1], -mine[:, 0]], axis=1)], axis=1)
    partial_value = jnp.einsum(
        "corit,crjt->coij", left, corr_volts, preferred_element_type=jnp.float32
    )
    partial_value = partial_value * (1.0 / (samples * n_time))
    columns = inputs_all // n_time
    vis_block = lax.psum_scatter(partial_value, "tm", scatter_dimension=3, tiled=True)
    gains = prior_gains
    for iteration in range(ITERS):
        power = jnp.sum(gains * gains, axis=(1, 2)) + 1e-06
        along = lax.dynamic_slice_in_dim(gains, time_index * columns, columns, 2)
        real_real = jnp.einsum("cij,cj->ci", vis_block[:, 0], along[:, 0], precision=highest)
        imag_imag = jnp.einsum("cij,cj->ci", vis_block[:, 1], along[:, 1], precision=highest)
        real_imag = jnp.einsum("cij,cj->ci", vis_block[:, 0], along[:, 1], precision=highest)
        imag_real = jnp.einsum("cij,cj->ci", vis_block[:, 1], along[:, 0], precision=highest)
        update = jnp.stack([real_real - imag_imag, imag_real + real_imag], axis=1)
        update = lax.psum(update, "tm")
        own_rows = lax.dynamic_slice_in_dim(gains, row_start, rows, 2)
        fresh = 0.5 * (own_rows + inputs_all * update / power[:, None, None])
        gains = lax.all_gather(fresh, "grp", axis=2, tiled=True)
    all_gains = lax.all_gather(gains, "freq", axis=0, tiled=True)
    my_beam = lax.dynamic_slice_in_dim(beam_channels, freq_index * per_device, per_device, 0)
    onehot = (corr_channels[None, :] == my_beam[:, None]).astype(jnp.float32)
    selected = jnp.einsum("ck,kri->cri", onehot, all_gains, precision=highest)
    ratio = 0.875 + 0.25 * (my_beam.astype(jnp.float32) + 0.5) / channels_all
    beams_mine = pointing.shape[1] // n_group
    pointing_part = lax.dynamic_slice_in_dim(pointing, group_index * beams_mine, beams_mine, 1)
    slot_coords = jnp.take(station_coords, ingest_map, axis=1)
    weights = jax.vmap(weights_for, in_axes=(0, 0, None, None))(
        selected, ratio, pointing_part, slot_coords
    )
    block = beam_volts.reshape(per_device, 2, 2, S, samples)
    beams = jnp.einsum("cpobrq,crpqt->cpobt", weights, block, preferred_element_type=jnp.float32)
    return (vis_block, gains, beams.astype(jnp.bfloat16))


def solution(mesh):
    return jax.shard_map(
        body,
        mesh=mesh,
        in_specs=(
            P(None, None, ("freq", "grp"), "tm"),
            P("freq", None, None),
            P(),
            P(),
            P(),
            P(),
            P(),
            P(),
        ),
        out_specs=(
            P("freq", None, "grp", "tm"),
            P("freq", None, None),
            P("freq", None, None, "grp", "tm"),
        ),
        check_vma=False,
    )
```

profile of v0, /device:TPU:1, one launch (start us, length us, event | category | flops | bytes accessed | tf_op | source)
XLA Modules:
  0.0 446.5 jit_solution(17262730501101874338)
XLA Ops:
  7.2 0.7 all-gather.2.cloned.1.call-update
  7.9 0.7 compare_select_fusion.1
  8.6 0.7 compare_and_fusion
  9.3 66.2 %all-gather.2.cloned.1.call-done = bf16[32,2,32,1024]{3,2,1,0:T(8,128)(2,1)} async-done(((bf16[32,2,16,1024]{3,2,1,0:T(8,128)(2,1)}), bf16[32,2,32,1024]{3,2,1,0:T(8,128)(2,1)}) %all-gather.2.cloned.1.call-update) | async-done | bytes 4194320 | tf_op jit(solution)/shard_map/all_gather | solution.py:60
  75.5 5.0 %gather_fusion.2 = bf16[32,2,32,1024]{3,2,1,0:T(8,128)(2,1)} fusion(bf16[32,2,32,1024]{3,2,1,0:T(8,128)(2,1)} %all-gather.2.cloned.1.call-done, s32[1024]{0:T(1024)S(1)} %pad_clamp_fusion.2), kind=kCustom, calls=%fused_computation.clone | custom fusion | bytes 8388736 | tf_op jit(solution)/shard_map/jit(_take)/gather | solution.py:61
  80.4 4.6 %broadcast_select_fusion.1 = bf16[32,2,32,1024]{3,2,1,0:T(8,128)(2,1)} fusion(bf16[32,2,32,1024]{3,2,1,0:T(8,128)(2,1)} %gather_fusion.2, pred[32]{0:T(512)(128)(4,1)S(1)} %get-tuple-element.27), kind=kLoop, calls=%fused_computation.14 | loop fusion | flops 2097152 | bytes 8388640 | tf_op jit(solution)/shard_map/jit(_take)/select_n | solution.py:61
  85.1 10.2 %all-to-all-start = ((bf16[32,2,32,1024]{3,2,1,0:T(8,128)(2,1)}), bf16[32,2,32,1024]{3,2,1,0:T(8,128)(2,1)}, u32[]{:S(2)}, u32[]{:S(2)}) async-start(bf16[32,2,32,1024]{3,2,1,0:T(8,128)(2,1)} %broadcast_select_fusion.1), calls=%async_computation | async-start | bytes 8388608 | tf_op jit(solution)/shard_map/all_to_all | solution.py:64
  95.3 3.5 gather_fusion
  98.9 0.1 convert_element_type.46
  99.0 0.1 dynamic-slice
  99.1 5.0 %gather_fusion.3 = bf16[32,2,32,1024]{3,2,1,0:T(8,128)(2,1)} fusion(bf16[32,2,32,1024]{3,2,1,0:T(8,128)(2,1)} %all-gather.2.cloned.1.call-done, s32[1024]{0:T(1024)S(1)} %pad_clamp_fusion), kind=kCustom, calls=%fused_computation.1.clone | custom fusion | bytes 8388736 | tf_op jit(solution)/shard_map/jit(_take)/gather | solution.py:62
  104.1 87.4 %all-to-all-done = bf16[32,2,32,1024]{3,2,1,0:T(8,128)(2,1)} async-done(((bf16[32,2,32,1024]{3,2,1,0:T(8,128)(2,1)}), bf16[32,2,32,1024]{3,2,1,0:T(8,128)(2,1)}, u32[]{:S(2)}, u32[]{:S(2)}) %all-to-all-start) | async-done | bytes 4194336 | tf_op jit(solution)/shard_map/all_to_all | solution.py:64
  191.4 2.6 copy.23
  194.0 0.4 dynamic-slice_multiply_fusion
  194.5 0.4 fusion.76
  194.9 2.5 broadcast_multiply_fusion
  197.4 0.8 copy.24
  198.2 0.1 fusion.74
  198.4 0.2 maximum_bitcast_fusion.4
  198.6 6.1 %fusion.5 = f32[1,2,512,1024]{3,2,1,0:T(8,128)} fusion(bf16[2,1024,1024,1]{2,1,0,3:T(8,128)(2,1)S(1)} %bitcast.170, bf16[1,1,2,512,1024]{4,3,2,1,0:T(8,128)(2,1)S(1)} %maximum_bitcast_fusion.4, bf16[1,1,2,512,1024]{4,3,2,1,0:T(8,128)(2,1)S(1)} %fusion.76), kind=kOutput, calls=%fused_computation.11 | convolution fusion | flops 4298113024 | bytes 12582912 | tf_op jit(solution)/shard_map/corit,crjt->coij/dot_general | solution.py:75
  204.7 4.6 %broadcast_select_fusion = bf16[32,2,32,1024]{3,2,1,0:T(8,128)(2,1)} fusion(bf16[32,2,32,1024]{3,2,1,0:T(8,128)(2,1)} %gather_fusion.3, pred[32]{0:T(512)(128)(4,1)S(1)} %get-tuple-element.26), kind=kLoop, calls=%fused_computation.13 | loop fusion | flops 2097152 | bytes 8388640 | tf_op jit(solution)/shard_map/jit(_take)/select_n | solution.py:62
  209.4 7.4 %all-to-all-start.1 = ((bf16[32,2,32,1024]{3,2,1,0:T(8,128)(2,1)}), bf16[32,2,32,1024]{3,2,1,0:T(8,128)(2,1)}, u32[]{:S(2)}, u32[]{:S(2)}) async-start(bf16[32,2,32,1024]{3,2,1,0:T(8,128)(2,1)} %broadcast_select_fusion), calls=%async_computation.2 | async-start | bytes 8388608 | tf_op jit(solution)/shard_map/all_to_all | solution.py:65
  216.8 0.6 dynamic_slice.42
  217.4 0.1 copy.25
  217.6 1.0 gather_fusion.1
  219.3 0.6 multiply_reduce_fusion.3
  220.6 0.1 select_bitcast_fusion
  220.7 0.3 slice_reduce_fusion.1
  221.0 1.0 fusion.34
  222.1 90.9 %all-to-all-done.1 = bf16[32,2,32,1024]{3,2,1,0:T(8,128)(2,1)} async-done(((bf16[32,2,32,1024]{3,2,1,0:T(8,128)(2,1)}), bf16[32,2,32,1024]{3,2,1,0:T(8,128)(2,1)}, u32[]{:S(2)}, u32[]{:S(2)}) %all-to-all-start.1) | async-done | bytes 4194336 | tf_op jit(solution)/shard_map/all_to_all | solution.py:65
  313.0 5.0 %copy.27 = bf16[1,2,32,32,1024]{4,3,2,1,0:T(8,128)(2,1)} copy(bf16[1,2,32,32,1024]{4,3,1,2,0:T(8,128)(2,1)} %bitcast.74) | data formatting | bytes 8388608 | tf_op jit(solution)/shard_map/all_to_all | solution.py:65
  317.9 1.7 fusion.29
  319.6 1.6 fusion.21
  321.2 1.6 fusion.22
  322.8 1.6 fusion.30
  324.5 8.4 %psum.28 = f32[1,2,512]{2,1,0:T(2,128)S(1)} all-reduce(f32[1,2,512]{2,1,0:T(2,128)S(1)} %pad_maximum_fusion), channel_id=1, replica_groups=mesh['freq'=32,'tm'=4,'grp'=2] {'tm'}, use_global_device_ids=true, to_apply=%region_1.3 | all-reduce | flops 1024 | bytes 8192 | tf_op jit(solution)/shard_map/psum | solution.py:90
  332.9 3.4 all_gather.19
  336.2 0.6 multiply_reduce_fusion.2
  336.9 1.6 fusion.27
  338.4 1.6 fusion.19
  340.0 1.6 fusion.20
  341.6 1.6 fusion.28
  343.3 6.0 %psum.29 = f32[1,2,512]{2,1,0:T(2,128)S(1)} all-reduce(f32[1,2,512]{2,1,0:T(2,128)S(1)} %pad_maximum_fusion.1), channel_id=1, replica_groups=mesh['freq'=32,'tm'=4,'grp'=2] {'tm'}, use_global_device_ids=true, to_apply=%region_3.5 | all-reduce | flops 1024 | bytes 8192 | tf_op jit(solution)/shard_map/psum | solution.py:90
  350.0 3.2 all_gather.20
  353.2 0.6 multiply_reduce_fusion.1
  353.8 0.5 fusion.25
  354.3 0.6 fusion.17
  354.9 0.6 fusion.18
  355.4 0.6 fusion.26
  356.0 7.4 %psum.30 = f32[1,2,512]{2,1,0:T(2,128)S(1)} all-reduce(f32[1,2,512]{2,1,0:T(2,128)S(1)} %pad_maximum_fusion.2), channel_id=1, replica_groups=mesh['freq'=32,'tm'=4,'grp'=2] {'tm'}, use_global_device_ids=true, to_apply=%region_5.7 | all-reduce | flops 1024 | bytes 8192 | tf_op jit(solution)/shard_map/psum | solution.py:90
  364.1 3.4 all_gather.21
  367.5 0.6 multiply_reduce_fusion
  368.1 0.5 fusion.23
  368.7 0.6 fusion.15
  369.2 0.6 fusion.16
  369.8 0.6 fusion.24
  370.4 6.0 %psum.31 = f32[1,2,512]{2,1,0:T(2,128)S(1)} all-reduce(f32[1,2,512]{2,1,0:T(2,128)S(1)} %pad_maximum_fusion.3), channel_id=1, replica_groups=mesh['freq'=32,'tm'=4,'grp'=2] {'tm'}, use_global_device_ids=true, to_apply=%region_7.9 | all-reduce | flops 1024 | bytes 8192 | tf_op jit(solution)/shard_map/psum | solution.py:90
  377.1 3.2 all_gather.22
  380.3 52.9 %all_gather.23 = f32[32,2,1024]{2,1,0:T(2,128)S(1)} all-gather(f32[1,2,1024]{2,1,0:T(2,128)S(1)} %all_gather.22), channel_id=1, replica_groups=mesh['freq'=32,'tm'=4,'grp'=2] {'freq'}, dimensions={0}, use_global_device_ids=true | all-gather | bytes 270336 | tf_op jit(solution)/shard_map/all_gather | solution.py:94
  433.2 0.9 fusion.31
  434.2 0.2 negate_convert_fusion
  434.4 0.1 maximum_bitcast_fusion.5
  434.5 4.6 %fusion.8 = bf16[1,2,2,128,1024]{4,3,2,1,0:T(8,128)(2,1)} fusion(bf16[2,1,128,2,512]{4,2,3,1,0:T(8,128)(2,1)S(1)} %get-tuple-element.17, bf16[2,1,128,2,512]{4,2,3,1,0:T(8,128)(2,1)S(1)} %get-tuple-element.16, bf16[2,2,512,1024]{3,2,1,0:T(8,128)(2,1)} %bitcast.169, bf16[2,512]{1,0:T(2,128)(2,1)S(1)} %convert_element_type.50), kind=kOutput, calls=%fused_computation.19 | convolution fusion | flops 1076887552 | bytes 6293504 | tf_op jit(solution)/shard_map/cpobrq,crpqt->cpobt/dot_general | solution.py:106
  439.1 0.6 copy.47
  (50 shorter events, 0.5 us)
Async XLA Ops:
  7.2 88.2 %copy-start = (s32[512]{0:T(512)S(1)}, s32[512]{0:T(512)}, u32[]{:S(2)}) copy-start(s32[512]{0:T(512)} %param.12) | copy-start | bytes 6148
  7.2 68.3 %all-gather.2.cloned.1.call-start = ((), (), s32[]{:S(2)}) async-start(), calls=%async_computation.3 | async-start | bytes 6291456 | tf_op jit(solution)/shard_map/all_gather | solution.py:60
  85.1 10.2 %copy-start.3 = (s32[512]{0:T(512)S(1)}, s32[512]{0:T(512)}, u32[]{:S(2)}) copy-start(s32[512]{0:T(512)} %param.13) | copy-start | bytes 6148
  85.1 106.3 %all-to-all-start = ((bf16[32,2,32,1024]{3,2,1,0:T(8,128)(2,1)}), bf16[32,2,32,1024]{3,2,1,0:T(8,128)(2,1)}, u32[]{:S(2)}, u32[]{:S(2)}) async-start(bf16[32,2,32,1024]{3,2,1,0:T(8,128)(2,1)} %broadcast_select_fusion.1), calls=%async_computation | async-start | bytes 8388608 | tf_op jit(solution)/shard_map/all_to_all | solution.py:64
  95.2 222.7 %reduce-scatter.2.cloned.1.call-start = ((), (), s32[]{:S(2)}) async-start(), calls=%async_computation.4 | async-start | bytes 5242880 | tf_op jit(solution)/shard_map/reduce_scatter | solution.py:80
  209.4 7.5 %copy-start.6 = (s32[32]{0:T(128)S(1)}, s32[32]{0:T(128)}, u32[]{:S(2)}) copy-start(s32[32]{0:T(128)} %param.17) | copy-start | bytes 388
  209.4 8.1 %copy-start.5 = (f32[2,512]{1,0:T(2,128)S(1)}, f32[2,512]{1,0:T(2,128)}, u32[]{:S(2)}) copy-start(f32[2,512]{1,0:T(2,128)} %param.14) | copy-start | bytes 12292
  209.4 9.9 %copy-start.2 = (f32[1,2,1024]{2,1,0:T(2,128)S(1)}, f32[1,2,1024]{2,1,0:T(2,128)}, u32[]{:S(2)}) copy-start(f32[1,2,1024]{2,1,0:T(2,128)} %param.11) | copy-start | bytes 24580
  209.4 11.2 %copy-start.7 = (s32[2,256]{1,0:T(2,128)S(1)}, s32[2,256]{1,0:T(2,128)}, u32[]{:S(2)}) copy-start(s32[2,256]{1,0:T(2,128)} %param.15) | copy-start | bytes 6148
  209.4 103.6 %all-to-all-start.1 = ((bf16[32,2,32,1024]{3,2,1,0:T(8,128)(2,1)}), bf16[32,2,32,1024]{3,2,1,0:T(8,128)(2,1)}, u32[]{:S(2)}, u32[]{:S(2)}) async-start(bf16[32,2,32,1024]{3,2,1,0:T(8,128)(2,1)} %broadcast_select_fusion), calls=%async_computation.2 | async-start | bytes 8388608 | tf_op jit(solution)/shard_map/all_to_all | solution.py:65
  317.9 35.8 %copy-start.1 = (f32[1,2,512,256]{3,2,1,0:T(8,128)S(1)}, f32[1,2,512,256]{3,2,1,0:T(8,128)}, u32[]{:S(2)}) copy-start(f32[1,2,512,256]{3,2,1,0:T(8,128)} %reduce-scatter.2.cloned.1.call-done) | copy-start | bytes 3145732
  319.6 113.6 %copy-start.4 = (s32[32]{0:T(128)S(1)}, s32[32]{0:T(128)}, u32[]{:S(2)}) copy-start(s32[32]{0:T(128)} %param.16) | copy-start | bytes 388
Sparse Core Ops, SparseCore 0:
  9.8 65.6 all-gather.1
  204.8 47.6 reduce-scatter.1
where the time goes:
time: 448 us; the launch traced here: 446 us
  waiting for transfers between devices  245 us (55%)
  blocking collectives  94 us (21%)
  matrix products  28.9 us (6%)
  local copies, waits for them, and re-layouts  24.8 us (6%)
  other arithmetic  18.4 us (4%)
  starting transfers between devices  17.7 us (4%)
  between operations  17.6 us (4%)
    all_to_all x1, waiting for transfers between devices, body(): lax.all_to_all(beam_source, 'freq', split_axis=0, concat_axis=2, tiled=True)  90.9 us
    all_to_all x1, waiting for transfers between devices, body(): lax.all_to_all(corr_source, 'freq', split_axis=0, concat_axis=2, tiled=True)  87.4 us
    all_gather x1, waiting for transfers between devices, body(): paired = lax.all_gather(voltages, 'grp', axis=2, tiled=True)  66.2 us
    all_gather x1, blocking collectives, body(): all_gains = lax.all_gather(gains, 'freq', axis=0, tiled=True)  52.9 us
    psum x4, blocking collectives, body(): update = lax.psum(update, 'tm')  27.9 us
    all_gather x4, blocking collectives, body(): gains = lax.all_gather(fresh, 'grp', axis=2, tiled=True)  13.2 us
    all_to_all x1, starting transfers between devices, body(): lax.all_to_all(corr_source, 'freq', split_axis=0, concat_axis=2, tiled=True)  10.2 us
  transfers between devices with their start and end apart: 4, of which 3 were waited for; matrix products, arithmetic and copies ran while one was open for 5% of the time, Pallas kernels for 0%

commit v1 on v0

--- a/solution.py
+++ b/solution.py
@@ -62,7 +62,15 @@
     beam_source = jnp.take(paired, beam_channels, axis=0)
     corr_volts, beam_volts = (
         lax.all_to_all(corr_source, "freq", split_axis=0, concat_axis=2, tiled=True),
-        lax.all_to_all(beam_source, "freq", split_axis=0, concat_axis=2, tiled=True),
+        jnp.concatenate(
+            jax.lax.all_to_all(
+                jnp.stack(jnp.split(beam_source, jax.lax.axis_size("freq"), 0), axis=0),
+                "freq",
+                0,
+                0,
+            ),
+            2,
+        ),
     )
     slot_keep = 1 - jnp.take(station_flags, ingest_map)
     keep = jnp.concatenate([slot_keep, slot_keep]).astype(jnp.bfloat16)

time: 448 us -> 446 us (level)
  local copies, waits for them, and re-layouts: 24.8 us -> 48.2 us
  waiting for transfers between devices: 245 us -> 222 us
    all_to_all x1, waiting for transfers between devices: 87.4 us -> 64.4 us  [body(): lax.all_to_all(corr_source, 'freq', split_axis=0, concat_axis=2, tiled=True)]
    unnamed x19 -> x54, local copies, waits for them, and re-layouts: 0.8 us -> 22.6 us
    reshape x0 -> x1, local copies, waits for them, and re-layouts: none -> 4.97 us  [body(): jnp.concatenate(jax.lax.all_to_all(jnp.stack(jnp.split(beam_source, jax.l...]
    all_to_all x1 -> x0, local copies, waits for them, and re-layouts: 4.97 us -> none  [body(): lax.all_to_all(beam_source, 'freq', split_axis=0, concat_axis=2, tiled=True)]
  transfers between devices with their start and end apart: 4 -> 4, of which waited for: 3 -> 3; matrix products, arithmetic and copies ran while one was open for 5% -> 10% of each run, Pallas kernels for 0% -> 0%
where the time goes in v1:
time: 446 us; the launch traced here: 445 us
  waiting for transfers between devices  222 us (50%)
  blocking collectives  93.8 us (21%)
  local copies, waits for them, and re-layouts  48.2 us (11%)
  matrix products  28.9 us (6%)
  starting transfers between devices  17.7 us (4%)
  between operations  17.7 us (4%)
  other arithmetic  16.4 us (4%)
    all_to_all x1, waiting for transfers between devices, body(): jax.lax.all_to_all(jnp.stack(jnp.split(beam_source, jax.lax.axis_size('fr...  90.9 us
    all_gather x1, waiting for transfers between devices, body(): paired = lax.all_gather(voltages, 'grp', axis=2, tiled=True)  66.2 us
    all_to_all x1, waiting for transfers between devices, body(): lax.all_to_all(corr_source, 'freq', split_axis=0, concat_axis=2, tiled=True)  64.4 us
    all_gather x1, blocking collectives, body(): all_gains = lax.all_gather(gains, 'freq', axis=0, tiled=True)  52.9 us
    psum x4, blocking collectives, body(): update = lax.psum(update, 'tm')  27.9 us
    unnamed x54, local copies, waits for them, and re-layouts  22.6 us
    all_gather x4, blocking collectives, body(): gains = lax.all_gather(fresh, 'grp', axis=2, tiled=True)  13 us
    all_to_all x1, starting transfers between devices, body(): lax.all_to_all(corr_source, 'freq', split_axis=0, concat_axis=2, tiled=True)  10.2 us
  transfers between devices with their start and end apart: 4, of which 3 were waited for; matrix products, arithmetic and copies ran while one was open for 10% of the time, Pallas kernels for 0%

profile of v1, /device:TPU:1, one launch (start us, length us, event | category | flops | bytes accessed | tf_op | source)
XLA Modules:
  0.0 444.9 jit_solution(367060601091566179)
XLA Ops:
  7.2 0.7 all-gather.2.cloned.1.call-update
  7.9 0.7 compare_select_fusion.1
  8.6 0.7 compare_and_fusion
  9.3 66.2 %all-gather.2.cloned.1.call-done = bf16[32,2,32,1024]{3,2,1,0:T(8,128)(2,1)} async-done(((bf16[32,2,16,1024]{3,2,1,0:T(8,128)(2,1)}), bf16[32,2,32,1024]{3,2,1,0:T(8,128)(2,1)}) %all-gather.2.cloned.1.call-update) | async-done | bytes 4194320 | tf_op jit(solution)/shard_map/all_gather | solution.py:60
  75.5 5.0 %gather_fusion.2 = bf16[32,2,32,1024]{3,2,1,0:T(8,128)(2,1)} fusion(bf16[32,2,32,1024]{3,2,1,0:T(8,128)(2,1)} %all-gather.2.cloned.1.call-done, s32[1024]{0:T(1024)S(1)} %pad_clamp_fusion.2), kind=kCustom, calls=%fused_computation.clone | custom fusion | bytes 8388736 | tf_op jit(solution)/shard_map/jit(_take)/gather | solution.py:61
  80.4 4.6 %broadcast_select_fusion.1 = bf16[32,2,32,1024]{3,2,1,0:T(8,128)(2,1)} fusion(bf16[32,2,32,1024]{3,2,1,0:T(8,128)(2,1)} %gather_fusion.2, pred[32]{0:T(512)(128)(4,1)S(1)} %get-tuple-element.27), kind=kLoop, calls=%fused_computation.14 | loop fusion | flops 2097152 | bytes 8388640 | tf_op jit(solution)/shard_map/jit(_take)/select_n | solution.py:61
  85.1 10.2 %all-to-all-start = ((bf16[32,2,32,1024]{3,2,1,0:T(8,128)(2,1)}), bf16[32,2,32,1024]{3,2,1,0:T(8,128)(2,1)}, u32[]{:S(2)}, u32[]{:S(2)}) async-start(bf16[32,2,32,1024]{3,2,1,0:T(8,128)(2,1)} %broadcast_select_fusion.1), calls=%async_computation | async-start | bytes 8388608 | tf_op jit(solution)/shard_map/all_to_all | solution.py:64
  95.3 3.5 gather_fusion
  99.1 5.0 %gather_fusion.3 = bf16[32,2,32,1024]{3,2,1,0:T(8,128)(2,1)} fusion(bf16[32,2,32,1024]{3,2,1,0:T(8,128)(2,1)} %all-gather.2.cloned.1.call-done, s32[1024]{0:T(1024)S(1)} %pad_clamp_fusion), kind=kCustom, calls=%fused_computation.1.clone | custom fusion | bytes 8388736 | tf_op jit(solution)/shard_map/jit(_take)/gather | solution.py:62
  104.1 2.6 broadcast_select_fusion
  106.7 0.7 fusion.66
  107.4 1.1 fusion.65
  108.6 0.7 fusion.64
  109.9 0.7 fusion.62
  110.5 0.7 fusion.61
  111.2 0.7 fusion.60
  111.9 0.7 fusion.59
  112.5 0.7 fusion.58
  113.2 0.7 fusion.57
  113.8 0.7 fusion.56
  114.5 0.7 fusion.55
  115.2 0.7 fusion.54
  115.8 0.7 fusion.53
  116.5 0.7 fusion.52
  117.1 0.7 fusion.51
  117.8 0.7 fusion.50
  118.4 0.7 fusion.49
  119.1 0.7 fusion.48
  119.8 0.7 fusion.47
  120.4 0.7 fusion.46
  121.1 0.7 fusion.45
  123.1 0.7 fusion.42
  123.7 0.7 fusion.41
  127.0 64.4 %all-to-all-done = bf16[32,2,32,1024]{3,2,1,0:T(8,128)(2,1)} async-done(((bf16[32,2,32,1024]{3,2,1,0:T(8,128)(2,1)}), bf16[32,2,32,1024]{3,2,1,0:T(8,128)(2,1)}, u32[]{:S(2)}, u32[]{:S(2)}) %all-to-all-start) | async-done | bytes 4194336 | tf_op jit(solution)/shard_map/all_to_all | solution.py:64
  191.4 2.6 copy.54
  194.9 2.5 broadcast_multiply_fusion
  197.4 0.8 copy.55
  198.6 6.2 %fusion.5 = f32[1,2,512,1024]{3,2,1,0:T(8,128)} fusion(bf16[2,1024,1024,1]{2,1,0,3:T(8,128)(2,1)S(1)} %bitcast.296, bf16[1,1,2,512,1024]{4,3,2,1,0:T(8,128)(2,1)S(1)} %maximum_bitcast_fusion.4, bf16[1,1,2,512,1024]{4,3,2,1,0:T(8,128)(2,1)S(1)} %fusion.108), kind=kOutput, calls=%fused_computation.11 | convolution fusion | flops 4298113024 | bytes 12582912 | tf_op jit(solution)/shard_map/corit,crjt->coij/dot_general | solution.py:83
  204.7 1.6 fusion.36
  206.3 1.6 fusion.35
  207.9 7.4 %all-to-all-start.1 = ((bf16[32,1,2,32,1024]{4,3,2,1,0:T(8,128)(2,1)}), bf16[32,1,2,32,1024]{4,3,2,1,0:T(8,128)(2,1)}, u32[]{:S(2)}, u32[]{:S(2)}) async-start(bf16[32,1,2,32,1024]{4,3,2,1,0:T(8,128)(2,1)} %fusion.35), calls=%async_computation.2 | async-start | bytes 8388608 | tf_op jit(solution)/shard_map/all_to_all | solution.py:66
  216.1 1.0 gather_fusion.1
  219.6 1.0 fusion.34
  220.6 90.9 %all-to-all-done.1 = bf16[32,1,2,32,1024]{4,3,2,1,0:T(8,128)(2,1)} async-done(((bf16[32,1,2,32,1024]{4,3,2,1,0:T(8,128)(2,1)}), bf16[32,1,2,32,1024]{4,3,2,1,0:T(8,128)(2,1)}, u32[]{:S(2)}, u32[]{:S(2)}) %all-to-all-start.1) | async-done | bytes 4194336 | tf_op jit(solution)/shard_map/all_to_all | solution.py:66
  311.5 5.0 %copy.58 = bf16[1,2,32,32,1024]{4,3,2,1,0:T(8,128)(2,1)} copy(bf16[1,2,32,32,1024]{4,3,1,0,2:T(8,128)(2,1)} %bitcast.105) | data formatting | bytes 8388608 | tf_op jit(solution)/shard_map/reshape | solution.py:65
  316.5 1.7 fusion.29
  318.1 1.6 fusion.21
  319.8 1.6 fusion.22
  321.4 1.6 fusion.30
  323.0 8.4 %psum.28 = f32[1,2,512]{2,1,0:T(2,128)S(1)} all-reduce(f32[1,2,512]{2,1,0:T(2,128)S(1)} %pad_maximum_fusion), channel_id=1, replica_groups=mesh['freq'=32,'tm'=4,'grp'=2] {'tm'}, use_global_device_ids=true, to_apply=%region_1.3 | all-reduce | flops 1024 | bytes 8192 | tf_op jit(solution)/shard_map/psum | solution.py:98
  331.4 3.2 all_gather.19
  335.2 1.6 fusion.27
  336.8 1.6 fusion.19
  338.4 1.6 fusion.20
  340.0 1.6 fusion.28
  341.6 6.0 %psum.29 = f32[1,2,512]{2,1,0:T(2,128)S(1)} all-reduce(f32[1,2,512]{2,1,0:T(2,128)S(1)} %pad_maximum_fusion.1), channel_id=1, replica_groups=mesh['freq'=32,'tm'=4,'grp'=2] {'tm'}, use_global_device_ids=true, to_apply=%region_3.5 | all-reduce | flops 1024 | bytes 8192 | tf_op jit(solution)/shard_map/psum | solution.py:98
  348.3 3.2 all_gather.20
  354.4 7.4 %psum.30 = f32[1,2,512]{2,1,0:T(2,128)S(1)} all-reduce(f32[1,2,512]{2,1,0:T(2,128)S(1)} %pad_maximum_fusion.2), channel_id=1, replica_groups=mesh['freq'=32,'tm'=4,'grp'=2] {'tm'}, use_global_device_ids=true, to_apply=%region_5.7 | all-reduce | flops 1024 | bytes 8192 | tf_op jit(solution)/shard_map/psum | solution.py:98
  362.5 3.4 all_gather.21
  368.7 6.0 %psum.31 = f32[1,2,512]{2,1,0:T(2,128)S(1)} all-reduce(f32[1,2,512]{2,1,0:T(2,128)S(1)} %pad_maximum_fusion.3), channel_id=1, replica_groups=mesh['freq'=32,'tm'=4,'grp'=2] {'tm'}, use_global_device_ids=true, to_apply=%region_7.9 | all-reduce | flops 1024 | bytes 8192 | tf_op jit(solution)/shard_map/psum | solution.py:98
  375.4 3.2 all_gather.22
  378.6 52.9 %all_gather.23 = f32[32,2,1024]{2,1,0:T(2,128)S(1)} all-gather(f32[1,2,1024]{2,1,0:T(2,128)S(1)} %all_gather.22), channel_id=1, replica_groups=mesh['freq'=32,'tm'=4,'grp'=2] {'freq'}, dimensions={0}, use_global_device_ids=true | all-gather | bytes 270336 | tf_op jit(solution)/shard_map/all_gather | solution.py:102
  431.6 0.9 fusion.31
  432.9 4.6 %fusion.8 = bf16[1,2,2,128,1024]{4,3,2,1,0:T(8,128)(2,1)} fusion(bf16[2,1,128,2,512]{4,2,3,1,0:T(8,128)(2,1)S(1)} %get-tuple-element.17, bf16[2,1,128,2,512]{4,2,3,1,0:T(8,128)(2,1)S(1)} %get-tuple-element.16, bf16[2,2,512,1024]{3,2,1,0:T(8,128)(2,1)} %bitcast.295, bf16[2,512]{1,0:T(2,128)(2,1)S(1)} %convert_element_type.50), kind=kOutput, calls=%fused_computation.19 | convolution fusion | flops 1076887552 | bytes 6293504 | tf_op jit(solution)/shard_map/cpobrq,crpqt->cpobt/dot_general | solution.py:114
  (86 shorter events, 15.2 us)
Async XLA Ops:
  7.2 88.2 %copy-start = (s32[512]{0:T(512)S(1)}, s32[512]{0:T(512)}, u32[]{:S(2)}) copy-start(s32[512]{0:T(512)} %param.12) | copy-start | bytes 6148
  7.2 68.3 %all-gather.2.cloned.1.call-start = ((), (), s32[]{:S(2)}) async-start(), calls=%async_computation.3 | async-start | bytes 6291456 | tf_op jit(solution)/shard_map/all_gather | solution.py:60
  85.1 10.2 %copy-start.5 = (s32[512]{0:T(512)S(1)}, s32[512]{0:T(512)}, u32[]{:S(2)}) copy-start(s32[512]{0:T(512)} %param.13) | copy-start | bytes 6148
  85.1 106.4 %all-to-all-start = ((bf16[32,2,32,1024]{3,2,1,0:T(8,128)(2,1)}), bf16[32,2,32,1024]{3,2,1,0:T(8,128)(2,1)}, u32[]{:S(2)}, u32[]{:S(2)}) async-start(bf16[32,2,32,1024]{3,2,1,0:T(8,128)(2,1)} %broadcast_select_fusion.1), calls=%async_computation | async-start | bytes 8388608 | tf_op jit(solution)/shard_map/all_to_all | solution.py:64
  95.2 221.2 %reduce-scatter.2.cloned.1.call-start = ((), (), s32[]{:S(2)}) async-start(), calls=%async_computation.4 | async-start | bytes 5242880 | tf_op jit(solution)/shard_map/reduce_scatter | solution.py:88
  106.7 19.6 %copy-start.3 = (bf16[32,2,32,1024]{3,2,1,0:T(8,128)(2,1)}, bf16[32,2,32,1024]{3,2,1,0:T(8,128)(2,1)S(1)}, u32[]{:S(2)}) copy-start(bf16[32,2,32,1024]{3,2,1,0:T(8,128)(2,1)S(1)} %broadcast_select_fusion) | copy-start | bytes 12582916
  207.9 7.5 %copy-start.8 = (s32[32]{0:T(128)S(1)}, s32[32]{0:T(128)}, u32[]{:S(2)}) copy-start(s32[32]{0:T(128)} %param.17) | copy-start | bytes 388
  207.9 8.1 %copy-start.7 = (f32[2,512]{1,0:T(2,128)S(1)}, f32[2,512]{1,0:T(2,128)}, u32[]{:S(2)}) copy-start(f32[2,512]{1,0:T(2,128)} %param.14) | copy-start | bytes 12292
  207.9 9.9 %copy-start.4 = (f32[1,2,1024]{2,1,0:T(2,128)S(1)}, f32[1,2,1024]{2,1,0:T(2,128)}, u32[]{:S(2)}) copy-start(f32[1,2,1024]{2,1,0:T(2,128)} %param.11) | copy-start | bytes 24580
  207.9 11.2 %copy-start.9 = (s32[2,256]{1,0:T(2,128)S(1)}, s32[2,256]{1,0:T(2,128)}, u32[]{:S(2)}) copy-start(s32[2,256]{1,0:T(2,128)} %param.15) | copy-start | bytes 6148
  207.9 103.6 %all-to-all-start.1 = ((bf16[32,1,2,32,1024]{4,3,2,1,0:T(8,128)(2,1)}), bf16[32,1,2,32,1024]{4,3,2,1,0:T(8,128)(2,1)}, u32[]{:S(2)}, u32[]{:S(2)}) async-start(bf16[32,1,2,32,1024]{4,3,2,1,0:T(8,128)(2,1)} %fusion.35), calls=%async_computation.2 | async-start | bytes 8388608 | tf_op jit(solution)/shard_map/all_to_all | solution.py:66
  316.5 35.7 %copy-start.2 = (f32[1,2,512,256]{3,2,1,0:T(8,128)S(1)}, f32[1,2,512,256]{3,2,1,0:T(8,128)}, u32[]{:S(2)}) copy-start(f32[1,2,512,256]{3,2,1,0:T(8,128)} %reduce-scatter.2.cloned.1.call-done) | copy-start | bytes 3145732
  318.1 113.4 %copy-start.6 = (s32[32]{0:T(128)S(1)}, s32[32]{0:T(128)}, u32[]{:S(2)}) copy-start(s32[32]{0:T(128)} %param.16) | copy-start | bytes 388
  432.8 5.2 %copy-start.1 = (s32[512]{0:T(512)S(1)}, s32[512]{0:T(512)}, u32[]{:S(2)}) copy-start(s32[512]{0:T(512)} %param.12) | copy-start | bytes 6148
Sparse Core Ops, SparseCore 0:
  9.8 65.6 all-gather.1
  204.9 47.6 reduce-scatter.1
